TPU v7x, 256 devices: a whole 4x4x8 slice. The times are simulated.
256 devices in a mesh: vocab: 64 (over y, z, core), hidden: 4 (over x).
Axes of the slice: x: 4, y: 4, z: 8, core: 2. Of those that a mesh axis runs over, the one named last changes fastest.
Arguments:
- states: bfloat16 [1024, 7168], P(('vocab', 'hidden')), may hold values from -32 to 32
- head: bfloat16 [7168, 129280], P('hidden', 'vocab'), may hold values from -1 to 1
Outputs:
- logp: float32 [1024, 129280], P('hidden', 'vocab')
All inputs are finite; a program needn't handle non-finite values.
Results may differ from a plain program's by a relative error of at most 0.0003.
Values may be sent and summed in bfloat16 or wider, within the bound.
A program may use at most 128 MiB of HBM per device.

v0:
```python
import math
import jax
import jax.numpy as jnp
from jax import lax
from jax.sharding import Mesh
from jax.sharding import PartitionSpec as P

VOCAB = ("vocab_0", "vocab_1", "vocab_2")
VOCAB_HIDDEN = ("vocab_0", "vocab_1", "vocab_2", "hidden")
sharpness = 4.0
minp_offset = math.log(10.0)
logp_floor = 30.0


def joined_along(pieces, dim):
    pieces = jnp.moveaxis(pieces, 0, dim)
    dims = pieces.shape
    return pieces.reshape(*dims[:dim], dims[dim] * dims[dim + 1], *dims[dim + 2 :])


def gather_in_order(shard, axes, order):
    pieces = shard
    for k in order:
        pieces = lax.all_gather(pieces, axes[k])
    done = order[::-1]
    back = [done.index(k) for k in range(len(axes))]
    pieces = pieces.transpose(*back, *range(len(axes), pieces.ndim))
    return pieces.reshape(-1, *shard.shape)


def gather_axes(shard, axes, order, dim):
    return joined_along(gather_in_order(shard, axes, order), dim)


def from_everyone(shard, axis):
    devices = lax.axis_size(axis)
    return lax.all_to_all(
        jnp.broadcast_to(shard[None], (devices, *shard.shape)), axis, 0, 0, tiled=True
    )


def over_copies(shard, axis):
    return from_everyone(shard, axis).max(axis=0)


def over_copies_2(shard, axis):
    return from_everyone(shard, axis).sum(axis=0)


def filtered(logits, top):
    shifted = logits - top[:, None]
    return shifted + jax.nn.log_sigmoid(sharpness * (shifted + minp_offset))


def body(states, head):
    slices = lax.all_to_all(states, "hidden", split_axis=1, concat_axis=0, tiled=True)
    gathered = gather_axes(slices, VOCAB, (0, 1, 2), 0)
    logits = lax.psum_scatter(
        jnp.dot(gathered, head, preferred_element_type=jnp.float32),
        "hidden",
        scatter_dimension=0,
        tiled=True,
    )
    top = over_copies(jnp.max(logits, axis=1), VOCAB)
    gated = filtered(logits, top)
    total = over_copies_2(jnp.sum(jnp.exp(gated), axis=1), VOCAB)
    return jnp.maximum(gated - jnp.log(total)[:, None], -logp_floor)


def solution(mesh):
    torus = Mesh(
        mesh.devices.reshape(4, 8, 2, mesh.shape["hidden"]),
        ("vocab_0", "vocab_1", "vocab_2", "hidden"),
    )
    return jax.shard_map(
        body,
        mesh=torus,
        in_specs=(P(VOCAB_HIDDEN, None), P("hidden", VOCAB)),
        out_specs=P("hidden", VOCAB),
        check_vma=False,
    )
```

profile of v0, /device:TPU:1, one launch (start us, length us, event | category | flops | bytes accessed | tf_op | source)
XLA Modules:
  0.0 236.1 jit_solution(12771082451407229781)
XLA Ops:
  6.5 0.0 all-gather.5.cloned.1.call-start
  6.5 9.3 %all_to_all.28 = bf16[4,4,1792]{2,0,1:T(4,128)(2,1)S(1)} all-to-all(bf16[4,4,1792]{2,0,1:T(4,128)(2,1)} %bitcast.13), channel_id=1, replica_groups=mesh['vocab_0'=4,'vocab_1'=8,'vocab_2'=2,'hidden'=4] {'hidden'}, dimensions={1} | all-to-all | bytes 114688 | tf_op jit(solution)/shard_map/all_to_all | solution.py:56
  15.8 10.6 %all_gather.19 = bf16[4,16,1792]{2,1,0:T(8,128)(2,1)} all-gather(bf16[1,16,1792]{2,1,0:T(8,128)(2,1)S(1)} %all_gather.18), channel_id=1, replica_groups=mesh['vocab_0'=4,'vocab_1'=8,'vocab_2'=2,'hidden'=4] {'vocab_0'}, dimensions={0}, use_global_device_ids=true | all-gather | bytes 286720 | tf_op jit(solution)/shard_map/all_gather | solution.py:24
  26.4 0.0 all-gather.5.cloned.1.call-update
  26.4 0.0 all-gather.7.cloned.1.call-start
  26.5 41.7 %all-gather.5.cloned.1.call-done = bf16[32,16,1792]{2,1,0:T(8,128)(2,1)} async-done(((bf16[4,16,1792]{2,1,0:T(8,128)(2,1)}), bf16[32,16,1792]{2,1,0:T(8,128)(2,1)}) %all-gather.5.cloned.1.call-update) | async-done | bytes 1835024 | tf_op jit(solution)/shard_map/all_gather | solution.py:24
  68.2 0.0 all-gather.7.cloned.1.call-update
  68.2 0.0 reduce-scatter.2.cloned.1.call-start
  68.3 23.0 %all-gather.7.cloned.1.call-done = bf16[16,4,16,1792]{3,2,1,0:T(8,128)(2,1)} async-done(((bf16[8,4,16,1792]{3,2,1,0:T(8,128)(2,1)}), bf16[16,4,16,1792]{3,2,1,0:T(8,128)(2,1)}) %all-gather.7.cloned.1.call-update) | async-done | bytes 3670032 | tf_op jit(solution)/shard_map/all_gather | solution.py:24
  91.3 0.0 copy-start.1
  91.3 2.6 %copy.11 = bf16[4,8,2,16,1792]{4,3,2,1,0:T(8,128)(2,1)S(1)} copy(bf16[4,8,2,16,1792]{4,3,0,1,2:T(8,128)(2,1)} %bitcast.9) | data formatting | bytes 7340032 | tf_op jit(solution)/shard_map/transpose | solution.py:27
  93.9 1.6 copy-done.1
  95.4 10.3 %fusion.2 = f32[1024,2020]{0,1:T(8,128)} fusion(bf16[1024,1792]{1,0:T(8,128)(2,1)S(1)} %bitcast.10, bf16[1792,2020]{0,1:T(8,128)(2,1)S(1)} %copy-done.1), kind=kOutput, calls=%fused_computation.5 | convolution fusion | flops 7413432320 | bytes 19183616 | tf_op jit(solution)/shard_map/dot_general | solution.py:59
  105.7 0.0 reduce-scatter.2.cloned.1.call-update
  105.7 83.2 %reduce-scatter.2.cloned.1.call-done = f32[256,2020]{0,1:T(8,128)} async-done(((f32[1024,2020]{0,1:T(8,128)}), f32[256,2020]{0,1:T(8,128)}) %reduce-scatter.2.cloned.1.call-update) | async-done | bytes 2068496 | tf_op jit(solution)/shard_map/reduce_scatter | solution.py:58
  188.9 0.0 copy-start
  188.9 2.0 reduce_max.18
  191.0 20.2 %all_to_all.29 = f32[64,1,256]{2,1,0:T(1,128)S(1)} all-to-all(f32[64,1,256]{2,1,0:T(1,128)S(1)} %broadcast_in_dim.4), channel_id=1, replica_groups=mesh['vocab_0'=4,'vocab_1'=8,'vocab_2'=2,'hidden'=4] {'vocab_0','vocab_1..., dimensions={0} | all-to-all | bytes 131072 | tf_op jit(solution)/shard_map/all_to_all | solution.py:37
  211.2 0.1 reduce_max.19
  211.3 0.0 copy-done
  211.3 1.6 exponential_reduce_fusion
  213.0 13.6 %all_to_all.30 = f32[64,1,256]{2,1,0:T(1,128)S(1)} all-to-all(f32[64,1,256]{2,1,0:T(1,128)S(1)} %broadcast_in_dim.5), channel_id=1, replica_groups=mesh['vocab_0'=4,'vocab_1'=8,'vocab_2'=2,'hidden'=4] {'vocab_0','vocab_1..., dimensions={0} | all-to-all | bytes 131072 | tf_op jit(solution)/shard_map/all_to_all | solution.py:37
  226.6 0.1 reduce_sum.19
  226.7 2.9 %subtract_maximum_fusion = f32[256,2020]{0,1:T(8,128)} fusion(f32[256]{0:T(256)S(1)} %log.7, f32[256,2020]{0,1:T(8,128)S(1)} %copy-done, f32[256]{0:T(256)S(1)} %reduce_max.19), kind=kLoop, calls=%fused_computation.3 | loop fusion | flops 7239680 | bytes 4139008 | tf_op jit(solution)/shard_map/max | solution.py:67
  (4 shorter events, 0.1 us)
Async XLA Ops:
  6.5 61.7 %all-gather.5.cloned.1.call-start = ((), (), s32[]{:S(2)}) async-start(), calls=%async_computation.5 | async-start | bytes 2064384 | tf_op jit(solution)/shard_map/all_gather | solution.py:24
  26.4 64.9 %all-gather.7.cloned.1.call-start = ((), (), s32[]{:S(2)}) async-start(), calls=%async_computation.6 | async-start | bytes 5505024 | tf_op jit(solution)/shard_map/all_gather | solution.py:24
  68.2 120.7 %reduce-scatter.2.cloned.1.call-start = ((), (), s32[]{:S(2)}) async-start(), calls=%async_computation.4 | async-start | bytes 10362880 | tf_op jit(solution)/shard_map/reduce_scatter | solution.py:58
  91.3 4.2 %copy-start.1 = (bf16[1792,2020]{0,1:T(8,128)(2,1)S(1)}, bf16[1792,2020]{0,1:T(8,128)(2,1)}, u32[]{:S(2)}) copy-start(bf16[1792,2020]{0,1:T(8,128)(2,1)} %param.3) | copy-start | bytes 21719044
  188.9 22.4 %copy-start = (f32[256,2020]{0,1:T(8,128)S(1)}, f32[256,2020]{0,1:T(8,128)}, u32[]{:S(2)}) copy-start(f32[256,2020]{0,1:T(8,128)} %reduce-scatter.2.cloned.1.call-done) | copy-start | bytes 6205444
Sparse Core Ops, SparseCore 0:
  26.5 41.6 all-gather.4
  70.0 21.2 all-gather.6
  105.9 82.9 reduce-scatter.1
where the time goes:
time: 236 us
  waiting for transfers between devices  148 us (63%)
  blocking collectives  53.7 us (23%)
  between operations  13.1 us (6%)
  matrix products  10.3 us (4%)
  other arithmetic  6.69 us (3%)
  local copies, waits for them, and re-layouts  4.26 us (2%)
    reduce_scatter x1, waiting for transfers between devices, body(): lax.psum_scatter(jnp.dot(gathered, head, preferred_element_type=jnp.float...  83.2 us
    all_gather x2, waiting for transfers between devices, gather_in_order(): pieces = lax.all_gather(pieces, axes[k])  64.7 us
    all_to_all x2, blocking collectives, from_everyone(): lax.all_to_all(jnp.broadcast_to(shard[None], (devices, *shard.shape)), ax...  33.9 us
    all_gather x1, blocking collectives, gather_in_order(): pieces = lax.all_gather(pieces, axes[k])  10.6 us
    dot_general x1, matrix products, body(): jnp.dot(gathered, head, preferred_element_type=jnp.float32)  10.3 us
    all_to_all x1, blocking collectives, body(): lax.all_to_all(states, 'hidden', split_axis=1, concat_axis=0, tiled=True)  9.27 us
  transfers between devices with their start and end apart: 3, of which 3 were waited for; matrix products, arithmetic and copies ran while one was open for 0% of the time, Pallas kernels for 0%

commit v1 on v0

--- a/solution.py
+++ b/solution.py
@@ -53,7 +53,9 @@
 
 
 def body(states, head):
-    slices = lax.all_to_all(states, "hidden", split_axis=1, concat_axis=0, tiled=True)
+    parts = jnp.split(states, lax.axis_size("hidden"), axis=1)
+    arrived = lax.all_to_all(jnp.stack(parts), "hidden", 0, 0)
+    slices = jnp.concatenate(arrived, axis=0)
     gathered = gather_axes(slices, VOCAB, (0, 1, 2), 0)
     logits = lax.psum_scatter(
         jnp.dot(gathered, head, preferred_element_type=jnp.float32),

time: 236 us -> 237 us (level)
  no operation moved by 1% of the time
where the time goes in v1:
time: 237 us
  waiting for transfers between devices  148 us (62%)
  blocking collectives  53.5 us (23%)
  between operations  13.1 us (6%)
  matrix products  10.3 us (4%)
  other arithmetic  6.74 us (3%)
  local copies, waits for them, and re-layouts  5.05 us (2%)
    reduce_scatter x1, waiting for transfers between devices, body(): lax.psum_scatter(jnp.dot(gathered, head, preferred_element_type=jnp.float...  83.2 us
    all_gather x2, waiting for transfers between devices, gather_in_order(): pieces = lax.all_gather(pieces, axes[k])  64.7 us
    all_to_all x2, blocking collectives, from_everyone(): lax.all_to_all(jnp.broadcast_to(shard[None], (devices, *shard.shape)), ax...  33.8 us
    all_gather x1, blocking collectives, gather_in_order(): pieces = lax.all_gather(pieces, axes[k])  10.6 us
    dot_general x1, matrix products, body(): jnp.dot(gathered, head, preferred_element_type=jnp.float32)  10.3 us
    all_to_all x1, blocking collectives, body(): arrived = lax.all_to_all(jnp.stack(parts), 'hidden', 0, 0)  9.08 us
  transfers between devices with their start and end apart: 3, of which 3 were waited for; matrix products, arithmetic and copies ran while one was open for 0% of the time, Pallas kernels for 0%

profile of v1, /device:TPU:1, one launch (start us, length us, event | category | flops | bytes accessed | tf_op | source)
XLA Modules:
  0.0 236.7 jit_solution(7088764140589157440)
XLA Ops:
  6.5 0.0 all-gather.5.cloned.1.call-start
  6.5 0.8 slice_bitcast_fusion.3
  7.3 0.1 pad_maximum_fusion
  7.4 9.1 %all_to_all.17 = bf16[4,4,1792]{2,1,0:T(4,128)(2,1)S(1)} all-to-all(bf16[4,4,1792]{2,1,0:T(4,128)(2,1)S(1)} %pad_maximum_fusion), channel_id=1, replica_groups=mesh['vocab_0'=4,'vocab_1'=8,'vocab_2'=2,'hidden'=4] {'hidden'}, dimensions={0} | all-to-all | bytes 114688 | tf_op jit(solution)/shard_map/all_to_all | solution.py:57
  16.5 10.6 %all_gather.15 = bf16[4,16,1792]{2,1,0:T(8,128)(2,1)} all-gather(bf16[1,16,1792]{2,1,0:T(8,128)(2,1)S(1)} %all_gather_reshape.3), channel_id=1, replica_groups=mesh['vocab_0'=4,'vocab_1'=8,'vocab_2'=2,'hidden'=4] {'vocab_0'}, dimensions={0}, use_global_device_ids=true | all-gather | bytes 286720 | tf_op jit(solution)/shard_map/all_gather | solution.py:24
  27.0 0.0 all-gather.5.cloned.1.call-update
  27.1 0.0 all-gather.7.cloned.1.call-start
  27.1 41.7 %all-gather.5.cloned.1.call-done = bf16[32,16,1792]{2,1,0:T(8,128)(2,1)} async-done(((bf16[4,16,1792]{2,1,0:T(8,128)(2,1)}), bf16[32,16,1792]{2,1,0:T(8,128)(2,1)}) %all-gather.5.cloned.1.call-update) | async-done | bytes 1835024 | tf_op jit(solution)/shard_map/all_gather | solution.py:24
  68.8 0.0 all-gather.7.cloned.1.call-update
  68.9 0.0 reduce-scatter.2.cloned.1.call-start
  68.9 23.0 %all-gather.7.cloned.1.call-done = bf16[16,4,16,1792]{3,2,1,0:T(8,128)(2,1)} async-done(((bf16[8,4,16,1792]{3,2,1,0:T(8,128)(2,1)}), bf16[16,4,16,1792]{3,2,1,0:T(8,128)(2,1)}) %all-gather.7.cloned.1.call-update) | async-done | bytes 3670032 | tf_op jit(solution)/shard_map/all_gather | solution.py:24
  91.9 0.0 copy-start.1
  91.9 2.6 %copy.6 = bf16[4,8,2,16,1792]{4,3,2,1,0:T(8,128)(2,1)S(1)} copy(bf16[4,8,2,16,1792]{4,3,0,1,2:T(8,128)(2,1)} %bitcast.15) | data formatting | bytes 7340032 | tf_op jit(solution)/shard_map/transpose | solution.py:27
  94.5 1.6 copy-done.1
  96.1 10.3 %fusion.2 = f32[1024,2020]{0,1:T(8,128)} fusion(bf16[1024,1792]{1,0:T(8,128)(2,1)S(1)} %bitcast.16, bf16[1792,2020]{0,1:T(8,128)(2,1)S(1)} %copy-done.1), kind=kOutput, calls=%fused_computation.10 | convolution fusion | flops 7413432320 | bytes 19183616 | tf_op jit(solution)/shard_map/dot_general | solution.py:61
  106.4 0.0 reduce-scatter.2.cloned.1.call-update
  106.4 83.2 %reduce-scatter.2.cloned.1.call-done = f32[256,2020]{0,1:T(8,128)} async-done(((f32[1024,2020]{0,1:T(8,128)}), f32[256,2020]{0,1:T(8,128)}) %reduce-scatter.2.cloned.1.call-update) | async-done | bytes 2068496 | tf_op jit(solution)/shard_map/reduce_scatter | solution.py:60
  189.6 0.0 copy-start
  189.6 2.0 reduce_max.18
  191.6 20.2 %all_to_all.18 = f32[64,1,256]{2,1,0:T(1,128)S(1)} all-to-all(f32[64,1,256]{2,1,0:T(1,128)S(1)} %broadcast_in_dim.4), channel_id=1, replica_groups=mesh['vocab_0'=4,'vocab_1'=8,'vocab_2'=2,'hidden'=4] {'vocab_0','vocab_1..., dimensions={0} | all-to-all | bytes 131072 | tf_op jit(solution)/shard_map/all_to_all | solution.py:37
  211.8 0.1 reduce_max.19
  211.9 0.0 copy-done
  211.9 1.6 exponential_reduce_fusion
  213.6 13.6 %all_to_all.19 = f32[64,1,256]{2,1,0:T(1,128)S(1)} all-to-all(f32[64,1,256]{2,1,0:T(1,128)S(1)} %broadcast_in_dim.5), channel_id=1, replica_groups=mesh['vocab_0'=4,'vocab_1'=8,'vocab_2'=2,'hidden'=4] {'vocab_0','vocab_1..., dimensions={0} | all-to-all | bytes 131072 | tf_op jit(solution)/shard_map/all_to_all | solution.py:37
  227.3 0.1 reduce_sum.19
  227.4 2.9 %subtract_maximum_fusion = f32[256,2020]{0,1:T(8,128)} fusion(f32[256]{0:T(256)S(1)} %log.7, f32[256,2020]{0,1:T(8,128)S(1)} %copy-done, f32[256]{0:T(256)S(1)} %reduce_max.19), kind=kLoop, calls=%fused_computation.3 | loop fusion | flops 7239680 | bytes 4139008 | tf_op jit(solution)/shard_map/max | solution.py:69
  (4 shorter events, 0.1 us)
Async XLA Ops:
  6.5 62.3 %all-gather.5.cloned.1.call-start = ((), (), s32[]{:S(2)}) async-start(), calls=%async_computation.5 | async-start | bytes 2064384 | tf_op jit(solution)/shard_map/all_gather | solution.py:24
  27.1 64.9 %all-gather.7.cloned.1.call-start = ((), (), s32[]{:S(2)}) async-start(), calls=%async_computation.6 | async-start | bytes 5505024 | tf_op jit(solution)/shard_map/all_gather | solution.py:24
  68.9 120.7 %reduce-scatter.2.cloned.1.call-start = ((), (), s32[]{:S(2)}) async-start(), calls=%async_computation.4 | async-start | bytes 10362880 | tf_op jit(solution)/shard_map/reduce_scatter | solution.py:60
  91.9 4.2 %copy-start.1 = (bf16[1792,2020]{0,1:T(8,128)(2,1)S(1)}, bf16[1792,2020]{0,1:T(8,128)(2,1)}, u32[]{:S(2)}) copy-start(bf16[1792,2020]{0,1:T(8,128)(2,1)} %param.3) | copy-start | bytes 21719044
  189.6 22.4 %copy-start = (f32[256,2020]{0,1:T(8,128)S(1)}, f32[256,2020]{0,1:T(8,128)}, u32[]{:S(2)}) copy-start(f32[256,2020]{0,1:T(8,128)} %reduce-scatter.2.cloned.1.call-done) | copy-start | bytes 6205444
Sparse Core Ops, SparseCore 0:
  27.2 41.6 all-gather.4
  70.6 21.2 all-gather.6
  106.5 83.0 reduce-scatter.1
